TPU v7x, 768 devices: a whole 4x8x12 slice. The times are simulated.
768 devices in a mesh: dp: 16 (over z_hi, y), ctx: 48 (over z_lo, x, core).
Axes of the slice: x: 4, y: 8, z: 12 (z_hi: 2, z_lo: 6; z = z_hi * 6 + z_lo), core: 2. Of those that a mesh axis runs over, the one named last changes fastest.
Arguments:
- queries: bfloat16 [48, 2048, 2560], P('ctx', 'dp'), may hold values from -20 to 20
- key_states: bfloat16 [48, 2048, 2560], P('ctx', 'dp'), may hold values from -20 to 20
- values: bfloat16 [48, 2048, 2560], P('ctx', 'dp'), may hold values from -6 to 6
- out_grad: bfloat16 [48, 2048, 2560], P('ctx', 'dp'), may hold values from -6 to 6
- block_links: int32 [2, 16], P(None, 'dp'), may hold values from -1 to 14, as said below
- sink_logit: float32 [20], replicated, may hold values from 4 to 8
Outputs:
- query_grad: bfloat16 [48, 2048, 2560], P('ctx', 'dp')
- key_grad: bfloat16 [48, 2048, 2560], P('ctx', 'dp')
- value_grad: bfloat16 [48, 2048, 2560], P('ctx', 'dp')
- sink_grad: float32 [20], replicated
Inputs may be any that keep to these rules, and one draw needn't show every extreme that they name: block_links[j, b] is either -1 or b - 2**j; it is -1 wherever b - 2**j < 0; block_links[0, 15] is 14.
All inputs are finite; a program needn't handle non-finite values.
Results may differ from a plain program's by a relative error of at most 0.023.
Values may be sent and summed in bfloat16 or wider, within the bound.
A program may use at most 64 MiB of HBM per device.

v0:
```python
import jax
import jax.numpy as jnp
from jax import lax
from jax.sharding import PartitionSpec as P

BLOCK = 128
LEVELS = 2


NEG_FILL = -1e30


def from_behind(value, axis, steps):
    count = lax.axis_size(axis)
    initial, last = (max(0, -steps), min(count, count - steps))
    return lax.ppermute(value, axis, [(source, source + steps) for source in range(initial, last)])


def causal_table(block_len):
    rows_iota = lax.broadcasted_iota(jnp.int32, (block_len, block_len), 0)
    cols_iota = lax.broadcasted_iota(jnp.int32, (block_len, block_len), 1)
    return rows_iota >= cols_iota


def attend_forward(q_blocks, key_all, val_all, allowed, sink_logit, score_scale):
    scores = (
        jnp.einsum("bqhd,bkhd->bhqk", q_blocks, key_all, preferred_element_type=jnp.float32)
        * score_scale
    )
    scores = jnp.where(allowed[:, None], scores, NEG_FILL)
    row_max = jnp.maximum(jnp.max(scores, axis=-1), sink_logit[None, :, None])
    exp_scores = jnp.exp(scores - row_max[..., None])
    sink_exp = jnp.exp(sink_logit[None, :, None] - row_max)
    denominator = jnp.sum(exp_scores, axis=-1) + sink_exp
    soft_prob = exp_scores / denominator[..., None]
    sink_prob = sink_exp / denominator
    weights = soft_prob.astype(jnp.bfloat16)
    output = jnp.einsum(
        "bhqk,bkhd->bqhd", weights, val_all, preferred_element_type=jnp.float32
    ).astype(jnp.bfloat16)
    return (soft_prob, weights, sink_prob, output)


def attend_backward(
    q_blocks, key_all, val_all, grad_blocks, soft_prob, weights, sink_prob, output, score_scale
):
    row_delta = jnp.sum(grad_blocks.astype(jnp.float32) * output.astype(jnp.float32), axis=-1)
    row_delta = jnp.transpose(row_delta, (0, 2, 1))
    prob_grad = jnp.einsum(
        "bqhd,bkhd->bhqk", grad_blocks, val_all, preferred_element_type=jnp.float32
    )
    score_grad = (soft_prob * (prob_grad - row_delta[..., None])).astype(jnp.bfloat16)
    query_grad = (
        jnp.einsum("bhqk,bkhd->bqhd", score_grad, key_all, preferred_element_type=jnp.float32)
        * score_scale
    ).astype(jnp.bfloat16)
    key_terms = (
        jnp.einsum("bhqk,bqhd->bkhd", score_grad, q_blocks, preferred_element_type=jnp.float32)
        * score_scale
    )
    value_terms = jnp.einsum(
        "bhqk,bqhd->bkhd", weights, grad_blocks, preferred_element_type=jnp.float32
    )
    sink_term = -jnp.sum(sink_prob * row_delta, axis=(0, 2))
    return (query_grad, key_terms, value_terms, sink_term)


def body(queries, key_states, values, out_grad, block_links, sink_logit):
    tokens = queries.shape[1]
    width = queries.shape[2]
    blocks = tokens // BLOCK
    heads = sink_logit.shape[0]
    head_size = width // heads
    score_scale = head_size ** (-0.5)

    def to_blocks(array):
        return array.reshape(blocks, BLOCK, heads, head_size)

    q_blocks = to_blocks(queries)
    grad_blocks = to_blocks(out_grad)
    level_live = block_links >= 0
    causal = jnp.broadcast_to(causal_table(BLOCK), (blocks, BLOCK, BLOCK))
    remote_masks = [
        jnp.broadcast_to(level_live[level_num][:, None, None], (blocks, BLOCK, BLOCK))
        for level_num in range(LEVELS)
    ]
    allowed = jnp.concatenate([causal] + remote_masks, axis=2)
    fetched = []
    for level_num in range(LEVELS):
        fetched.append(from_behind((key_states, values), "dp", 2**level_num))
    key_all = jnp.concatenate(
        [to_blocks(key_states)] + [to_blocks(moved[0]) for moved in fetched], axis=1
    )
    val_all = jnp.concatenate(
        [to_blocks(values)] + [to_blocks(moved[1]) for moved in fetched], axis=1
    )
    soft_prob, weights, sink_prob, output = attend_forward(
        q_blocks, key_all, val_all, allowed, sink_logit, score_scale
    )
    refetched = []
    for level_num in range(LEVELS):
        refetched.append(from_behind((key_states, values), "dp", 2**level_num))
    key_all = jnp.concatenate(
        [to_blocks(key_states)] + [to_blocks(moved[0]) for moved in refetched], axis=1
    )
    val_all = jnp.concatenate(
        [to_blocks(values)] + [to_blocks(moved[1]) for moved in refetched], axis=1
    )
    query_grad, key_terms, value_terms, sink_term = attend_backward(
        q_blocks, key_all, val_all, grad_blocks, soft_prob, weights, sink_prob, output, score_scale
    )
    key_grad = key_terms[:, :BLOCK].reshape(1, tokens, width)
    value_grad = value_terms[:, :BLOCK].reshape(1, tokens, width)
    for level_num in range(LEVELS):
        first_col = BLOCK * (1 + level_num)
        key_part = (
            key_terms[:, first_col : first_col + BLOCK]
            .reshape(1, tokens, width)
            .astype(jnp.bfloat16)
        )
        value_part = (
            value_terms[:, first_col : first_col + BLOCK]
            .reshape(1, tokens, width)
            .astype(jnp.bfloat16)
        )
        key_back, value_back = from_behind((key_part, value_part), "dp", -(2**level_num))
        key_grad = key_grad + key_back.astype(jnp.float32)
        value_grad = value_grad + value_back.astype(jnp.float32)
    sink_grad = lax.psum(sink_term, ("dp", "ctx"))
    return (
        query_grad.reshape(1, tokens, width),
        key_grad.astype(jnp.bfloat16),
        value_grad.astype(jnp.bfloat16),
        sink_grad,
    )


def solution(mesh):
    placed = (
        P("ctx", "dp", None),
        P("ctx", "dp", None),
        P("ctx", "dp", None),
        P("ctx", "dp", None),
        P(None, "dp"),
        P(),
    )
    return jax.shard_map(
        body,
        mesh=mesh,
        in_specs=placed,
        out_specs=(P("ctx", "dp", None), P("ctx", "dp", None), P("ctx", "dp", None), P()),
        check_vma=False,
    )
```

profile of v0, /device:TPU:312, one launch (start us, length us, event | category | flops | bytes accessed | tf_op | source)
XLA Modules:
  0.0 552.7 jit_solution(17386648955286758059)
XLA Ops:
  2.1 11.3 %collective-permute-start.3 = (bf16[1,128,2560]{1,2,0:T(8,128)(2,1)S(1)}, bf16[1,128,2560]{1,2,0:T(8,128)(2,1)}, u32[]{:S(2)}, u32[]{:S(2)}) collective-permute-start(bf16[1,128,2560]{1,2,0:T(8,128)(2,1)S(1)} %copy.34), channel_id=1, source_target_pairs={{0,96},{48,144},{96,192},{144,240},{192,288},{240,336},{288,384},{... | collective-permute-start | bytes 1966088 | tf_op jit(solution)/shard_map/ppermute | solution.py:16
  13.4 3.5 collective-permute-start.2
  18.3 5.7 %collective-permute-start.1 = (bf16[1,128,2560]{1,2,0:T(8,128)(2,1)S(1)}, bf16[1,128,2560]{1,2,0:T(8,128)(2,1)}, u32[]{:S(2)}, u32[]{:S(2)}) collective-permute-start(bf16[1,128,2560]{1,2,0:T(8,128)(2,1)S(1)} %copy.26), channel_id=1, source_target_pairs={{0,96},{48,144},{96,192},{144,240},{192,288},{240,336},{288,384},{... | collective-permute-start | bytes 1966088 | tf_op jit(solution)/shard_map/ppermute | solution.py:16
  24.1 2.6 collective-permute-start
  34.1 138.7 %collective-permute-done.3 = bf16[1,128,2560]{1,2,0:T(8,128)(2,1)} collective-permute-done((bf16[1,128,2560]{1,2,0:T(8,128)(2,1)S(1)}, bf16[1,128,2560]{1,2,0:T(8,128)(2,1)}, u32[]{:S(2)}, u32[]{:S(2)}) %collective-permute-start.3) | collective-permute-done | bytes 655392 | tf_op jit(solution)/shard_map/ppermute | solution.py:16
  172.8 2.2 copy.39
  175.0 11.9 %collective-permute-done.2 = bf16[1,128,2560]{1,2,0:T(8,128)(2,1)} collective-permute-done((bf16[1,128,2560]{1,2,0:T(8,128)(2,1)S(1)}, bf16[1,128,2560]{1,2,0:T(8,128)(2,1)}, u32[]{:S(2)}, u32[]{:S(2)}) %collective-permute-start.2) | collective-permute-done | bytes 655392 | tf_op jit(solution)/shard_map/ppermute | solution.py:16
  186.9 2.2 copy.38
  189.0 11.9 %collective-permute-done.1 = bf16[1,128,2560]{1,2,0:T(8,128)(2,1)} collective-permute-done((bf16[1,128,2560]{1,2,0:T(8,128)(2,1)S(1)}, bf16[1,128,2560]{1,2,0:T(8,128)(2,1)}, u32[]{:S(2)}, u32[]{:S(2)}) %collective-permute-start.1) | collective-permute-done | bytes 655392 | tf_op jit(solution)/shard_map/ppermute | solution.py:16
  202.4 12.5 %collective-permute-done = bf16[1,128,2560]{1,2,0:T(8,128)(2,1)} collective-permute-done((bf16[1,128,2560]{1,2,0:T(8,128)(2,1)S(1)}, bf16[1,128,2560]{1,2,0:T(8,128)(2,1)}, u32[]{:S(2)}, u32[]{:S(2)}) %collective-permute-start) | collective-permute-done | bytes 655392 | tf_op jit(solution)/shard_map/ppermute | solution.py:16
  220.4 1.9 fusion.6
  225.7 2.5 fusion.28
  228.3 106.1 %psum.7 = f32[20]{0:T(128)} all-reduce(f32[20]{0:T(128)S(1)} %neg.3), channel_id=1, replica_groups=mesh['dp'=16,'ctx'=48] {'dp','ctx'}, use_global_device_ids=true, to_apply=%region_4.5 | all-reduce | flops 20 | bytes 160 | tf_op jit(solution)/shard_map/psum | solution.py:129
  337.0 1.9 collective-permute-start.5
  338.9 1.9 collective-permute-start.4
  340.9 5.5 fusion.29
  348.9 3.9 collective-permute-start.7
  352.8 5.4 collective-permute-start.6
  360.0 2.5 slice.36
  362.5 1.7 copy.49
  364.2 93.3 %collective-permute-done.5 = bf16[1,128,2560]{1,2,0:T(8,128)(2,1)} collective-permute-done((bf16[1,128,2560]{1,2,0:T(8,128)(2,1)}, bf16[1,128,2560]{1,2,0:T(8,128)(2,1)}, u32[]{:S(2)}, u32[]{:S(2)}) %collective-permute-start.5) | collective-permute-done | bytes 655392 | tf_op jit(solution)/shard_map/ppermute | solution.py:16
  457.6 65.5 %collective-permute-done.4 = bf16[1,128,2560]{1,2,0:T(8,128)(2,1)} collective-permute-done((bf16[1,128,2560]{1,2,0:T(8,128)(2,1)S(1)}, bf16[1,128,2560]{1,2,0:T(8,128)(2,1)}, u32[]{:S(2)}, u32[]{:S(2)}) %collective-permute-start.4) | collective-permute-done | bytes 655392 | tf_op jit(solution)/shard_map/ppermute | solution.py:16
  525.8 24.6 %collective-permute-done.6 = bf16[1,128,2560]{2,1,0:T(8,128)(2,1)} collective-permute-done((bf16[1,128,2560]{2,1,0:T(8,128)(2,1)}, bf16[1,128,2560]{2,1,0:T(8,128)(2,1)}, u32[]{:S(2)}, u32[]{:S(2)}) %collective-permute-start.6) | collective-permute-done | bytes 655392 | tf_op jit(solution)/shard_map/ppermute | solution.py:16
  550.4 2.3 add_convert_fusion
  (65 shorter events, 30.2 us)
Async XLA Ops:
  0.6 27.4 %copy-start.1 = (bf16[1,128,2560]{2,1,0:T(8,128)(2,1)S(1)}, bf16[1,128,2560]{2,1,0:T(8,128)(2,1)}, u32[]{:S(2)}) copy-start(bf16[1,128,2560]{2,1,0:T(8,128)(2,1)} %param.9) | copy-start | bytes 1966084
  0.6 28.8 %copy-start.13 = (s32[2,1]{0,1:T(1,128)S(1)}, s32[2,1]{0,1:T(1,128)}, u32[]{:S(2)}) copy-start(s32[2,1]{0,1:T(1,128)} %param.10) | copy-start | bytes 28
  2.1 31.4 %copy-start.3 = (bf16[1,128,2560]{2,1,0:T(8,128)(2,1)S(1)}, bf16[1,128,2560]{2,1,0:T(8,128)(2,1)}, u32[]{:S(2)}) copy-start(bf16[1,128,2560]{2,1,0:T(8,128)(2,1)} %param.6) | copy-start | bytes 1966084
  2.1 170.7 %collective-permute-start.3 = (bf16[1,128,2560]{1,2,0:T(8,128)(2,1)S(1)}, bf16[1,128,2560]{1,2,0:T(8,128)(2,1)}, u32[]{:S(2)}, u32[]{:S(2)}) collective-permute-start(bf16[1,128,2560]{1,2,0:T(8,128)(2,1)S(1)} %copy.34), channel_id=1, source_target_pairs={{0,96},{48,144},{96,192},{144,240},{192,288},{240,336},{288,384},{... | collective-permute-start | bytes 1966088 | tf_op jit(solution)/shard_map/ppermute | solution.py:16
  13.4 173.4 %collective-permute-start.2 = (bf16[1,128,2560]{1,2,0:T(8,128)(2,1)S(1)}, bf16[1,128,2560]{1,2,0:T(8,128)(2,1)}, u32[]{:S(2)}, u32[]{:S(2)}) collective-permute-start(bf16[1,128,2560]{1,2,0:T(8,128)(2,1)S(1)} %copy.34), channel_id=1, source_target_pairs={{0,48},{48,96},{96,144},{144,192},{192,240},{240,288},{288,336},{3... | collective-permute-start | bytes 1966088 | tf_op jit(solution)/shard_map/ppermute | solution.py:16
  18.3 182.6 %collective-permute-start.1 = (bf16[1,128,2560]{1,2,0:T(8,128)(2,1)S(1)}, bf16[1,128,2560]{1,2,0:T(8,128)(2,1)}, u32[]{:S(2)}, u32[]{:S(2)}) collective-permute-start(bf16[1,128,2560]{1,2,0:T(8,128)(2,1)S(1)} %copy.26), channel_id=1, source_target_pairs={{0,96},{48,144},{96,192},{144,240},{192,288},{240,336},{288,384},{... | collective-permute-start | bytes 1966088 | tf_op jit(solution)/shard_map/ppermute | solution.py:16
  24.1 190.8 %collective-permute-start = (bf16[1,128,2560]{1,2,0:T(8,128)(2,1)S(1)}, bf16[1,128,2560]{1,2,0:T(8,128)(2,1)}, u32[]{:S(2)}, u32[]{:S(2)}) collective-permute-start(bf16[1,128,2560]{1,2,0:T(8,128)(2,1)S(1)} %copy.26), channel_id=1, source_target_pairs={{0,48},{48,96},{96,144},{144,192},{192,240},{240,288},{288,336},{3... | collective-permute-start | bytes 1966088 | tf_op jit(solution)/shard_map/ppermute | solution.py:16
  28.1 194.4 %copy-start.4 = (bf16[1,128,2560]{1,2,0:T(8,128)(2,1)}, bf16[1,128,2560]{1,2,0:T(8,128)(2,1)S(1)}, u32[]{:S(2)}) copy-start(bf16[1,128,2560]{1,2,0:T(8,128)(2,1)S(1)} %copy.40) | copy-start | bytes 1966084
  33.9 182.4 %copy-start.5 = (bf16[1,128,20,128]{3,1,2,0:T(8,128)(2,1)S(1)}, bf16[1,128,20,128]{3,1,2,0:T(8,128)(2,1)}, u32[]{:S(2)}) copy-start(bf16[1,128,20,128]{3,1,2,0:T(8,128)(2,1)} %copy.29) | copy-start | bytes 1966084
  202.3 14.0 %copy-start.9 = (bf16[1,128,20,128]{3,1,2,0:T(8,128)(2,1)}, bf16[1,128,20,128]{3,1,2,0:T(8,128)(2,1)S(1)}, u32[]{:S(2)}) copy-start(bf16[1,128,20,128]{3,1,2,0:T(8,128)(2,1)S(1)} %copy.31) | copy-start | bytes 1966084
  216.3 0.8 copy-start.12
  217.1 5.4 copy-start
  217.1 2.3 copy-start.2
  217.1 2.9 copy-start.6
  217.1 3.1 copy-start.7
  217.1 3.3 copy-start.8
  222.5 1.6 copy-start.10
  225.7 108.6 %copy-start.11 = (bf16[20,128,128]{2,1,0:T(8,128)(2,1)S(1)}, bf16[20,128,128]{2,1,0:T(8,128)(2,1)}, u32[]{:S(2)}) copy-start(bf16[20,128,128]{2,1,0:T(8,128)(2,1)} %fusion.4) | copy-start | bytes 1966084
  337.0 120.5 %collective-permute-start.5 = (bf16[1,128,2560]{1,2,0:T(8,128)(2,1)}, bf16[1,128,2560]{1,2,0:T(8,128)(2,1)}, u32[]{:S(2)}, u32[]{:S(2)}) collective-permute-start(bf16[1,128,2560]{1,2,0:T(8,128)(2,1)} %bitcast.31), channel_id=1, source_target_pairs={{96,0},{144,48},{192,96},{240,144},{288,192},{336,240},{384,288},{... | collective-permute-start | bytes 1966088 | tf_op jit(solution)/shard_map/ppermute | solution.py:16
  338.9 184.1 %collective-permute-start.4 = (bf16[1,128,2560]{1,2,0:T(8,128)(2,1)S(1)}, bf16[1,128,2560]{1,2,0:T(8,128)(2,1)}, u32[]{:S(2)}, u32[]{:S(2)}) collective-permute-start(bf16[1,128,2560]{1,2,0:T(8,128)(2,1)S(1)} %bitcast.124), channel_id=1, source_target_pairs={{48,0},{96,48},{144,96},{192,144},{240,192},{288,240},{336,288},{3... | collective-permute-start | bytes 1966088 | tf_op jit(solution)/shard_map/ppermute | solution.py:16
  348.9 176.9 %collective-permute-start.7 = (bf16[1,128,2560]{2,1,0:T(8,128)(2,1)}, bf16[1,128,2560]{2,1,0:T(8,128)(2,1)}, u32[]{:S(2)}, u32[]{:S(2)}) collective-permute-start(bf16[1,128,2560]{2,1,0:T(8,128)(2,1)} %copy.55), channel_id=1, source_target_pairs={{96,0},{144,48},{192,96},{240,144},{288,192},{336,240},{384,288},{... | collective-permute-start | bytes 1966088 | tf_op jit(solution)/shard_map/ppermute | solution.py:16
  352.8 197.6 %collective-permute-start.6 = (bf16[1,128,2560]{2,1,0:T(8,128)(2,1)}, bf16[1,128,2560]{2,1,0:T(8,128)(2,1)}, u32[]{:S(2)}, u32[]{:S(2)}) collective-permute-start(bf16[1,128,2560]{2,1,0:T(8,128)(2,1)} %copy.53), channel_id=1, source_target_pairs={{48,0},{96,48},{144,96},{192,144},{240,192},{288,240},{336,288},{3... | collective-permute-start | bytes 1966088 | tf_op jit(solution)/shard_map/ppermute | solution.py:16
where the time goes:
time: 553 us
  waiting for transfers between devices  358 us (65%)
  blocking collectives  106 us (19%)
  starting transfers between devices  36.1 us (7%)
  local copies, waits for them, and re-layouts  31.8 us (6%)
  matrix products  13.9 us (3%)
    ppermute x8, waiting for transfers between devices, from_behind(): lax.ppermute(value, axis, [(source, source + steps) for source in range(i...  358 us
    psum x1, blocking collectives, body(): sink_grad = lax.psum(sink_term, ('dp', 'ctx'))  106 us
    ppermute x8, starting transfers between devices, from_behind(): lax.ppermute(value, axis, [(source, source + steps) for source in range(i...  36.1 us
  transfers between devices with their start and end apart: 8, of which 7 were waited for; matrix products, arithmetic and copies ran while one was open for 6% of the time, Pallas kernels for 0%

commit v1 on v0

v1 whole, which is shorter than its diff:
```python
import functools

import jax
import jax.numpy as jnp
from jax import lax
from jax.experimental import pallas as pl
from jax.experimental.pallas import tpu as pltpu
from jax.sharding import PartitionSpec as P

MESH = pl.DeviceIdType.MESH
BLOCK = 128
HEAD = 128
CHUNKS = 10
AHEAD = 2
NEG_FILL = -1e30
CORES = 2


def body_kernel(
    dims,
    links,
    sink,
    q_ref,
    k_ref,
    v_ref,
    g_ref,
    dq_ref,
    dk_ref,
    dv_ref,
    sg_ref,
    kv1,
    kv2,
    rt1,
    rs0,
    st1,
    ss0,
    near,
    own,
    sink_rows,
    plane,
    column,
    row,
    up_send,
    up_recv,
    fw_send,
    fw_recv,
    t1_send,
    t1_recv,
    s0_send,
    s0_recv,
    re_send,
    plane_sem,
    column_sem,
    row_sem,
):
    n, n_ctx, heads = dims
    chunks = CHUNKS
    per = heads // chunks
    width = per * HEAD
    half = n // 2
    scale = HEAD**-0.5
    me = lax.axis_index("dp")
    ctx = lax.axis_index("ctx")
    last = n - 1
    is_lo = me == half - 1
    is_hi = me == half
    is_relay = (me == 0) | (me == last)
    relay_par = jnp.where(me == 0, 1, 0)

    n_plane = 8
    n_zlo = n_ctx // n_plane
    n_col = 2 * n_zlo
    pos_plane = lax.rem(ctx, n_plane)
    zlo = ctx // n_plane
    zhi = me // half
    y = lax.rem(me, half)
    pos_col = zhi * n_zlo + zlo

    def plane_peer(slot):
        return {"dp": me, "ctx": zlo * n_plane + slot}

    def column_peer(slot):
        return {
            "dp": (slot // n_zlo) * half + y,
            "ctx": lax.rem(slot, n_zlo) * n_plane + pos_plane,
        }

    def row_peer(slot):
        return {"dp": zhi * half + slot, "ctx": ctx}

    groups = (
        (n_plane, pos_plane, plane_peer, plane, plane_sem),
        (n_col, pos_col, column_peer, column, column_sem),
        (half, y, row_peer, row, row_sem),
    )

    barrier = pltpu.get_barrier_semaphore()
    total = 0
    for size, pos, peer, _, _ in groups:

        def greet(step, carry, size=size, pos=pos, peer=peer):
            pl.semaphore_signal(
                barrier, inc=1, device_id=peer(lax.rem(pos + step, size)), device_id_type=MESH
            )
            return carry

        lax.fori_loop(1, size, greet, 0)
        total += size - 1
    pl.semaphore_wait(barrier, total)

    def relay_of(c):
        return jnp.where(lax.rem(c, 2) == 0, last, 0)

    def up_device(c):
        return {"dp": jnp.where(is_lo, relay_of(c), jnp.minimum(me + 1, last)), "ctx": ctx}

    def down_device(c):
        return {"dp": jnp.where(is_hi, relay_of(c), jnp.maximum(me - 1, 0)), "ctx": ctx}

    def up_slot(c):
        return c + jnp.where(is_lo, chunks, 0)

    def down_slot(c):
        return c + jnp.where(is_hi, chunks, 0)

    def lanes(c):
        return pl.ds(pl.multiple_of(c * width, width), width)

    def copy(src, dst, send, recv, device):
        return pltpu.make_async_remote_copy(
            src_ref=src,
            dst_ref=dst,
            send_sem=send,
            recv_sem=recv,
            device_id=device,
            device_id_type=MESH,
        )

    def own_copies(c):
        slot = up_slot(c)
        return [
            copy(
                ref.at[:, lanes(c)],
                kv1.at[slot, which],
                up_send.at[c],
                up_recv.at[slot],
                up_device(c),
            )
            for which, ref in enumerate((k_ref, v_ref))
        ]

    def send_own(c):
        for each in own_copies(c):
            each.start()

    def fw_copy(c):
        slot = up_slot(c)
        return copy(kv1.at[c], kv2.at[slot], fw_send.at[c], fw_recv.at[slot], up_device(c))

    def t1_copy(c):
        slot = down_slot(c)
        return copy(st1.at[c], rt1.at[slot], t1_send.at[c], t1_recv.at[slot], down_device(c))

    def s0_copy(c):
        slot = down_slot(c)
        return copy(ss0.at[c], rs0.at[slot], s0_send.at[c], s0_recv.at[slot], down_device(c))

    def landed(ref, sem, slot):
        pltpu.make_async_copy(ref.at[slot], ref.at[slot], sem.at[slot]).wait()

    relays = (
        (kv1, up_recv, half),
        (kv2, fw_recv, half),
        (rt1, t1_recv, half - 1),
        (rs0, s0_recv, half - 1),
    )

    def relay_copy(which, c):
        ref, sem, target = relays[which]
        return copy(
            ref.at[chunks + c],
            ref.at[c],
            re_send.at[which, c],
            sem.at[c],
            {"dp": target, "ctx": ctx},
        )

    def relay(which, c):
        @pl.when(is_relay & (lax.rem(c, 2) == relay_par) & (c >= 0) & (c < chunks))
        def _():
            ref, sem, _ = relays[which]
            landed(ref, sem, chunks + c)
            relay_copy(which, c).start()

    has_down = me >= 1
    has_far = me >= 2
    has_up = me <= last - 1

    @pl.when(has_up)
    def _():
        for c in range(AHEAD):
            send_own(jnp.int32(c))

    zero = jnp.zeros((2, BLOCK, width), jnp.bfloat16)

    def clear(ref):
        def one(c, carry):
            ref[c] = zero
            return carry

        lax.fori_loop(0, chunks, one, 0)

    @pl.when(me == 0)
    def _():
        clear(kv1)

    @pl.when(me <= 1)
    def _():
        clear(kv2)

    @pl.when(me == last)
    def _():
        clear(rs0)
        clear(rt1)

    sink_rows[...] = jnp.zeros_like(sink_rows)
    bias = [jnp.where(links[level, 0] >= 0, 0.0, NEG_FILL) for level in range(2)]
    key_pos = lax.broadcasted_iota(jnp.int32, (BLOCK, BLOCK), 0)
    query_pos = lax.broadcasted_iota(jnp.int32, (BLOCK, BLOCK), 1)
    causal = query_pos >= key_pos

    def dot(a, b, dims):
        return lax.dot_general(a, b, (dims, ((), ())), preferred_element_type=jnp.float32)

    def attend(c):
        for i in range(per):
            head = c * per + i
            at = pl.ds(pl.multiple_of(c * width + i * HEAD, HEAD), HEAD)
            part = slice(i * HEAD, (i + 1) * HEAD)
            q = q_ref[:, at]
            g = g_ref[:, at]
            keys = (k_ref[:, at], kv1[c, 0, :, part], kv2[c, 0, :, part])
            vals = (v_ref[:, at], kv1[c, 1, :, part], kv2[c, 1, :, part])
            logit = sink[head]
            scores = [dot(k, q, ((1,), (1,))) * scale for k in keys]
            scores = [
                jnp.where(causal, scores[0], NEG_FILL),
                scores[1] + bias[0],
                scores[2] + bias[1],
            ]
            top = jnp.maximum(jnp.maximum(scores[0], scores[1]), scores[2])
            top = jnp.maximum(jnp.max(top, axis=0, keepdims=True), logit)
            exps = [jnp.exp(s - top) for s in scores]
            sink_exp = jnp.exp(logit - top)
            denom = jnp.sum(exps[0] + exps[1] + exps[2], axis=0, keepdims=True) + sink_exp
            inverse = 1.0 / denom
            probs = [e * inverse for e in exps]
            prob_grads = [dot(v, g, ((1,), (1,))) for v in vals]
            mixed = (
                probs[0] * prob_grads[0] + probs[1] * prob_grads[1] + probs[2] * prob_grads[2]
            )
            delta = jnp.sum(mixed, axis=0, keepdims=True)
            score_grads = [
                (p * (d - delta)).astype(jnp.bfloat16) for p, d in zip(probs, prob_grads)
            ]
            weights = [p.astype(jnp.bfloat16) for p in probs]
            sink_rows[pl.ds(head, 1), :] = -(sink_exp * inverse * delta)
            dq = dot(score_grads[0], keys[0], ((0,), (0,)))
            dq += dot(score_grads[1], keys[1], ((0,), (0,)))
            dq += dot(score_grads[2], keys[2], ((0,), (0,)))
            dq_ref[:, at] = (dq * scale).astype(jnp.bfloat16)
            own[c, 0, :, part] = dot(score_grads[0], q, ((1,), (0,))) * scale
            own[c, 1, :, part] = dot(weights[0], g, ((1,), (0,)))
            near[c, 0, :, part] = dot(score_grads[1], q, ((1,), (0,))) * scale
            near[c, 1, :, part] = dot(weights[1], g, ((1,), (0,)))
            st1[c, 0, :, part] = (dot(score_grads[2], q, ((1,), (0,))) * scale).astype(
                jnp.bfloat16
            )
            st1[c, 1, :, part] = dot(weights[2], g, ((1,), (0,))).astype(jnp.bfloat16)

    def pass_near(c):
        @pl.when(has_down & has_up)
        def _():
            landed(rt1, t1_recv, c)

        @pl.when(has_down)
        def _():
            ss0[c] = (near[c] + rt1[c].astype(jnp.float32)).astype(jnp.bfloat16)
            s0_copy(c).start()

    def finish(c):
        @pl.when(has_up)
        def _():
            landed(rs0, s0_recv, c)

        dk_ref[:, lanes(c)] = (own[c, 0] + rs0[c, 0].astype(jnp.float32)).astype(jnp.bfloat16)
        dv_ref[:, lanes(c)] = (own[c, 1] + rs0[c, 1].astype(jnp.float32)).astype(jnp.bfloat16)

    def step(c, carry):
        relay(0, c)

        @pl.when(has_down)
        def _():
            landed(kv1, up_recv, c)

        @pl.when(has_down & has_up)
        def _():
            fw_copy(c).start()

        @pl.when(has_up & (c + AHEAD < chunks))
        def _():
            send_own(c + AHEAD)

        relay(1, c)
        relay(2, c - 1)

        @pl.when(has_far)
        def _():
            landed(kv2, fw_recv, c)

        attend(c)

        @pl.when(has_far)
        def _():
            t1_copy(c).start()

        relay(3, c - 2)

        @pl.when(c >= 1)
        def _():
            pass_near(c - 1)

        @pl.when(c >= 3)
        def _():
            finish(c - 3)

        return carry

    lax.fori_loop(0, chunks, step, 0)

    def publish(which, value):
        size, pos, peer, buf, sem = groups[which]
        buf[pos] = value

        def one(s, carry):
            slot = lax.rem(pos + s, size)
            copy(buf.at[pos], buf.at[pos], sem.at[0, s], sem.at[1, pos], peer(slot)).start()
            return carry

        lax.fori_loop(1, size, one, 0)

    def collect(which):
        size, pos, peer, buf, sem = groups[which]

        def one(s, carry):
            slot = lax.rem(pos + s, size)
            pltpu.make_async_copy(buf.at[slot], buf.at[slot], sem.at[1, slot]).wait()
            pltpu.make_async_copy(buf.at[pos], buf.at[pos], sem.at[0, s]).wait()
            return carry

        lax.fori_loop(1, size, one, 0)
        out = buf[0]
        for s in range(1, size):
            out = out + buf[s]
        return out

    by_lane = jnp.sum(jnp.transpose(sink_rows[...]), axis=0, keepdims=True)
    publish(0, jnp.broadcast_to(by_lane, (8, 128)))
    relay(2, jnp.int32(chunks - 1))
    pass_near(jnp.int32(chunks - 1))
    publish(1, collect(0))
    relay(3, jnp.int32(chunks - 2))
    relay(3, jnp.int32(chunks - 1))
    finish(jnp.int32(chunks - 3))
    finish(jnp.int32(chunks - 2))
    publish(2, collect(1))
    finish(jnp.int32(chunks - 1))
    sg_ref[...] = collect(2)

    def drain(c, carry):
        @pl.when(has_up)
        def _():
            pltpu.make_async_copy(kv1.at[0], kv1.at[0], up_send.at[c]).wait()

        @pl.when(has_up & has_down)
        def _():
            pltpu.make_async_copy(kv1.at[0], kv1.at[0], fw_send.at[c]).wait()

        @pl.when(has_far)
        def _():
            pltpu.make_async_copy(st1.at[0], st1.at[0], t1_send.at[c]).wait()

        @pl.when(has_down)
        def _():
            pltpu.make_async_copy(ss0.at[0], ss0.at[0], s0_send.at[c]).wait()

        @pl.when(is_relay & (lax.rem(c, 2) == relay_par))
        def _():
            for which in range(4):
                pltpu.make_async_copy(kv1.at[0], kv1.at[0], re_send.at[which, c]).wait()

        return carry

    lax.fori_loop(0, chunks, drain, 0)


def solution(mesh):
    n, n_ctx = mesh.shape["dp"], mesh.shape["ctx"]

    def body(queries, key_states, values, out_grad, block_links, sink_logit):
        shape = queries.shape
        tokens, full = shape[1], shape[2]
        heads = sink_logit.shape[0]
        width = full // CHUNKS
        flat = [a.reshape(tokens, full) for a in (queries, key_states, values, out_grad)]
        vmem = pl.BlockSpec(memory_space=pltpu.VMEM)
        smem = pl.BlockSpec(memory_space=pltpu.SMEM)
        wide = pltpu.VMEM((2 * CHUNKS, 2, BLOCK, width), jnp.bfloat16)
        once = pltpu.VMEM((CHUNKS, 2, BLOCK, width), jnp.bfloat16)
        sums = pltpu.VMEM((CHUNKS, 2, BLOCK, width), jnp.float32)
        dma = pltpu.SemaphoreType.DMA
        n_col = 2 * (n_ctx // 8)
        dq, dk, dv, sg = pl.pallas_call(
            functools.partial(body_kernel, (n, n_ctx, heads)),
            out_shape=[jax.ShapeDtypeStruct((tokens, full), jnp.bfloat16)] * 3
            + [jax.ShapeDtypeStruct((8, 128), jnp.float32)],
            in_specs=[smem, smem] + [vmem] * 4,
            out_specs=[vmem] * 4,
            scratch_shapes=[
                wide,
                wide,
                wide,
                wide,
                once,
                once,
                sums,
                sums,
                pltpu.VMEM((128, 128), jnp.float32),
                pltpu.VMEM((8, 8, 128), jnp.float32),
                pltpu.VMEM((n_col, 8, 128), jnp.float32),
                pltpu.VMEM((n // 2, 8, 128), jnp.float32),
                dma((CHUNKS,)),
                dma((2 * CHUNKS,)),
                dma((CHUNKS,)),
                dma((2 * CHUNKS,)),
                dma((CHUNKS,)),
                dma((2 * CHUNKS,)),
                dma((CHUNKS,)),
                dma((2 * CHUNKS,)),
                dma((4, CHUNKS)),
                dma((2, 8)),
                dma((2, n_col)),
                dma((2, n // 2)),
            ],
            compiler_params=pltpu.CompilerParams(
                collective_id=0, has_side_effects=True, vmem_limit_bytes=50 * 1024 * 1024
            ),
        )(block_links, sink_logit, *flat)
        return dq.reshape(shape), dk.reshape(shape), dv.reshape(shape), sg[0, :heads]

    placed = (
        P("ctx", "dp", None),
        P("ctx", "dp", None),
        P("ctx", "dp", None),
        P("ctx", "dp", None),
        P(None, "dp"),
        P(),
    )
    return jax.shard_map(
        body,
        mesh=mesh,
        in_specs=placed,
        out_specs=(P("ctx", "dp", None), P("ctx", "dp", None), P("ctx", "dp", None), P()),
        check_vma=False,
    )
```

time: 553 us -> 246 us (0.44)
  the two profiles are of different devices: /device:TPU:312 before, /device:TPU:2 now
where the time goes in v1:
time: 246 us
  Pallas kernels  237 us (96%)
  local copies, waits for them, and re-layouts  7.58 us (3%)
    pallas_call x1, Pallas kernels, body(): pl.pallas_call(functools.partial(body_kernel, (n, n_ctx, heads)), out_sha...  237 us
    unnamed x14, local copies, waits for them, and re-layouts  7.07 us

profile of v1, /device:TPU:2, one launch (start us, length us, event | category | flops | bytes accessed | tf_op | source)
XLA Modules:
  0.0 245.7 jit_solution(5793319064997190427)
XLA Ops:
  0.6 0.0 copy-start.4
  0.6 0.6 copy-done.4
  1.3 0.0 copy-start.3
  1.3 0.1 copy.10.links
  1.4 0.6 copy-done.3
  1.9 0.0 copy-start
  1.9 1.1 copy-done
  3.0 0.0 copy-start.1
  3.0 1.1 copy-done.1
  4.1 0.0 copy-start.2
  4.1 1.1 copy-done.2
  5.2 237.4 %shard_map.93 = (bf16[128,2560]{1,0:T(8,128)(2,1)S(1)}, bf16[128,2560]{1,0:T(8,128)(2,1)S(1)}, bf16[128,2560]{1,0:T(8,128)(2,1)S(1)}, f32[8,128]{1,0:T(8,128)S(1)}) custom-call(s32[2,1]{1,0:T(2,128)S(1)} %copy.10.links, f32[20]{0:T(128)S(1)} %copy-done.3, bf16[128,2560]{1,0:T(8,128)(2,1)S(1)} %bitcast.12, bf16[128,2560]{1,0:T(8,128)(2,1)S(1)} %bitcast.13, ...), custom_call_target="tpu_custom_call" | custom-call | tf_op jit(solution)/shard_map/pallas_call | solution.py:423
  242.7 0.5 slice_bitcast_fusion
  243.2 0.8 copy.14
  244.0 0.8 copy.15
  244.8 0.8 copy.16
Async XLA Ops:
  0.6 0.7 copy-start.4
  1.3 0.7 copy-start.3
  1.9 1.1 copy-start
  3.0 1.1 copy-start.1
  4.1 1.1 copy-start.2

commit v2 on v1

--- a/solution.py
+++ b/solution.py
@@ -13,7 +13,10 @@
 CHUNKS = 10
 AHEAD = 2
 NEG_FILL = -1e30
-CORES = 2
+LAG_LO = 5
+LAG_T1 = 3
+LAG_S0 = 4
+LAG_END = 6
 
 
 def body_kernel(
@@ -65,7 +68,7 @@
     is_lo = me == half - 1
     is_hi = me == half
     is_relay = (me == 0) | (me == last)
-    relay_par = jnp.where(me == 0, 1, 0)
+    relay_half = jnp.where(me == 0, 1, 0)
 
     n_plane = 8
     n_zlo = n_ctx // n_plane
@@ -74,6 +77,7 @@
     zlo = ctx // n_plane
     zhi = me // half
     y = lax.rem(me, half)
+    across = lax.rem(zlo + n_zlo // 2, n_zlo) * n_plane + pos_plane
     pos_col = zhi * n_zlo + zlo
 
     def plane_peer(slot):
@@ -106,16 +110,30 @@
 
         lax.fori_loop(1, size, greet, 0)
         total += size - 1
-    pl.semaphore_wait(barrier, total)
-
-    def relay_of(c):
-        return jnp.where(lax.rem(c, 2) == 0, last, 0)
-
-    def up_device(c):
-        return {"dp": jnp.where(is_lo, relay_of(c), jnp.minimum(me + 1, last)), "ctx": ctx}
-
-    def down_device(c):
-        return {"dp": jnp.where(is_hi, relay_of(c), jnp.maximum(me - 1, 0)), "ctx": ctx}
+    is_edge = is_lo | is_hi | is_relay
+
+    @pl.when(is_edge)
+    def _():
+        facing = jnp.where(me < half, half - 1 - me, half + last - me)
+        pl.semaphore_signal(
+            barrier, inc=1, device_id={"dp": facing, "ctx": across}, device_id_type=MESH
+        )
+
+    pl.semaphore_wait(barrier, total + jnp.where(is_edge, 1, 0))
+
+    def up_device(which):
+        relay_dp = last if which == 0 else 0
+        return {
+            "dp": jnp.where(is_lo, relay_dp, jnp.minimum(me + 1, last)),
+            "ctx": jnp.where(is_lo, across, ctx),
+        }
+
+    def down_device(which):
+        relay_dp = last if which == 0 else 0
+        return {
+            "dp": jnp.where(is_hi, relay_dp, jnp.maximum(me - 1, 0)),
+            "ctx": jnp.where(is_hi, across, ctx),
+        }
 
     def up_slot(c):
         return c + jnp.where(is_lo, chunks, 0)
@@ -144,7 +162,7 @@
                 kv1.at[slot, which],
                 up_send.at[c],
                 up_recv.at[slot],
-                up_device(c),
+                up_device(which),
             )
             for which, ref in enumerate((k_ref, v_ref))
         ]
@@ -153,17 +171,20 @@
         for each in own_copies(c):
             each.start()
 
-    def fw_copy(c):
-        slot = up_slot(c)
-        return copy(kv1.at[c], kv2.at[slot], fw_send.at[c], fw_recv.at[slot], up_device(c))
-
-    def t1_copy(c):
-        slot = down_slot(c)
-        return copy(st1.at[c], rt1.at[slot], t1_send.at[c], t1_recv.at[slot], down_device(c))
-
-    def s0_copy(c):
-        slot = down_slot(c)
-        return copy(ss0.at[c], rs0.at[slot], s0_send.at[c], s0_recv.at[slot], down_device(c))
+    def pair(src, dst, send, recv, c, slot, device):
+        for which in range(2):
+            copy(
+                src.at[c, which], dst.at[slot, which], send.at[c], recv.at[slot], device(which)
+            ).start()
+
+    def send_fw(c):
+        pair(kv1, kv2, fw_send, fw_recv, c, up_slot(c), up_device)
+
+    def send_t1(c):
+        pair(st1, rt1, t1_send, t1_recv, c, down_slot(c), down_device)
+
+    def send_s0(c):
+        pair(ss0, rs0, s0_send, s0_recv, c, down_slot(c), down_device)
 
     def landed(ref, sem, slot):
         pltpu.make_async_copy(ref.at[slot], ref.at[slot], sem.at[slot]).wait()
@@ -175,22 +196,19 @@
         (rs0, s0_recv, half - 1),
     )
 
-    def relay_copy(which, c):
-        ref, sem, target = relays[which]
-        return copy(
-            ref.at[chunks + c],
-            ref.at[c],
-            re_send.at[which, c],
-            sem.at[c],
-            {"dp": target, "ctx": ctx},
-        )
-
-    def relay(which, c):
-        @pl.when(is_relay & (lax.rem(c, 2) == relay_par) & (c >= 0) & (c < chunks))
-        def _():
-            ref, sem, _ = relays[which]
-            landed(ref, sem, chunks + c)
-            relay_copy(which, c).start()
+    def relay(stream, c):
+        @pl.when(is_relay & (c >= 0) & (c < chunks))
+        def _():
+            ref, sem, target = relays[stream]
+            held = ref.at[chunks + c, relay_half]
+            pltpu.make_async_copy(held, held, sem.at[chunks + c]).wait()
+            copy(
+                held,
+                ref.at[c, relay_half],
+                re_send.at[stream, c],
+                sem.at[c],
+                {"dp": target, "ctx": across},
+            ).start()
 
     has_down = me >= 1
     has_far = me >= 2
@@ -198,7 +216,7 @@
 
     @pl.when(has_up)
     def _():
-        for c in range(AHEAD):
+        for c in range(AHEAD + 1):
             send_own(jnp.int32(c))
 
     zero = jnp.zeros((2, BLOCK, width), jnp.bfloat16)
@@ -286,7 +304,7 @@
         @pl.when(has_down)
         def _():
             ss0[c] = (near[c] + rt1[c].astype(jnp.float32)).astype(jnp.bfloat16)
-            s0_copy(c).start()
+            send_s0(c)
 
     def finish(c):
         @pl.when(has_up)
@@ -296,23 +314,31 @@
         dk_ref[:, lanes(c)] = (own[c, 0] + rs0[c, 0].astype(jnp.float32)).astype(jnp.bfloat16)
         dv_ref[:, lanes(c)] = (own[c, 1] + rs0[c, 1].astype(jnp.float32)).astype(jnp.bfloat16)
 
+    def forward(c):
+        @pl.when(has_down & (c < chunks))
+        def _():
+            landed(kv1, up_recv, c)
+
+        @pl.when(has_down & has_up & (c < chunks))
+        def _():
+            send_fw(c)
+
+    lag = jnp.where(is_lo, LAG_LO, 1)
+
+    def near_lagged(c):
+        @pl.when((c >= lag) & (c - lag < chunks))
+        def _():
+            pass_near(c - lag)
+
     def step(c, carry):
-        relay(0, c)
-
-        @pl.when(has_down)
-        def _():
-            landed(kv1, up_recv, c)
-
-        @pl.when(has_down & has_up)
-        def _():
-            fw_copy(c).start()
-
-        @pl.when(has_up & (c + AHEAD < chunks))
-        def _():
-            send_own(c + AHEAD)
+        relay(0, c + 1)
+        forward(c + 1)
+
+        @pl.when(has_up & (c + AHEAD + 1 < chunks))
+        def _():
+            send_own(c + AHEAD + 1)
 
         relay(1, c)
-        relay(2, c - 1)
 
         @pl.when(has_far)
         def _():
@@ -322,20 +348,20 @@
 
         @pl.when(has_far)
         def _():
-            t1_copy(c).start()
-
-        relay(3, c - 2)
-
-        @pl.when(c >= 1)
-        def _():
-            pass_near(c - 1)
-
-        @pl.when(c >= 3)
-        def _():
-            finish(c - 3)
+            send_t1(c)
+
+        relay(2, c - LAG_T1)
+        near_lagged(c)
+        relay(3, c - LAG_S0)
+
+        @pl.when(c >= LAG_END)
+        def _():
+            finish(c - LAG_END)
 
         return carry
 
+    relay(0, jnp.int32(0))
+    forward(jnp.int32(0))
     lax.fori_loop(0, chunks, step, 0)
 
     def publish(which, value):
@@ -366,15 +392,23 @@
 
     by_lane = jnp.sum(jnp.transpose(sink_rows[...]), axis=0, keepdims=True)
     publish(0, jnp.broadcast_to(by_lane, (8, 128)))
-    relay(2, jnp.int32(chunks - 1))
-    pass_near(jnp.int32(chunks - 1))
+
+    def tail(c, carry):
+        relay(2, c - LAG_T1)
+        near_lagged(c)
+        relay(3, c - LAG_S0)
+        return carry
+
+    lax.fori_loop(chunks, chunks + 1, tail, 0)
     publish(1, collect(0))
-    relay(3, jnp.int32(chunks - 2))
-    relay(3, jnp.int32(chunks - 1))
-    finish(jnp.int32(chunks - 3))
-    finish(jnp.int32(chunks - 2))
+    lax.fori_loop(chunks + 1, chunks + LAG_LO, tail, 0)
     publish(2, collect(1))
-    finish(jnp.int32(chunks - 1))
+
+    def ending(c, carry):
+        finish(c)
+        return carry
+
+    lax.fori_loop(chunks - LAG_END, chunks, ending, 0)
     sg_ref[...] = collect(2)
 
     def drain(c, carry):
@@ -394,10 +428,10 @@
         def _():
             pltpu.make_async_copy(ss0.at[0], ss0.at[0], s0_send.at[c]).wait()
 
-        @pl.when(is_relay & (lax.rem(c, 2) == relay_par))
+        @pl.when(is_relay)
         def _():
             for which in range(4):
-                pltpu.make_async_copy(kv1.at[0], kv1.at[0], re_send.at[which, c]).wait()
+                pltpu.make_async_copy(kv1.at[0, 0], kv1.at[0, 0], re_send.at[which, c]).wait()
 
         return carry
 

time: 246 us -> 182 us (0.74)
  the two profiles are of different devices: /device:TPU:2 before, /device:TPU:24 now
where the time goes in v2:
time: 182 us
  Pallas kernels  174 us (96%)
  local copies, waits for them, and re-layouts  7.58 us (4%)
    pallas_call x1, Pallas kernels, body(): pl.pallas_call(functools.partial(body_kernel, (n, n_ctx, heads)), out_sha...  174 us
    unnamed x14, local copies, waits for them, and re-layouts  7.07 us

profile of v2, /device:TPU:24, one launch (start us, length us, event | category | flops | bytes accessed | tf_op | source)
XLA Modules:
  0.0 181.8 jit_solution(8647509513036799396)
XLA Ops:
  0.6 0.0 copy-start.4
  0.6 0.6 copy-done.4
  1.3 0.0 copy-start.3
  1.3 0.1 copy.10.links
  1.4 0.6 copy-done.3
  1.9 0.0 copy-start
  1.9 1.1 copy-done
  3.0 0.0 copy-start.1
  3.0 1.1 copy-done.1
  4.1 0.0 copy-start.2
  4.1 1.1 copy-done.2
  5.2 173.6 %shard_map.93 = (bf16[128,2560]{1,0:T(8,128)(2,1)S(1)}, bf16[128,2560]{1,0:T(8,128)(2,1)S(1)}, bf16[128,2560]{1,0:T(8,128)(2,1)S(1)}, f32[8,128]{1,0:T(8,128)S(1)}) custom-call(s32[2,1]{1,0:T(2,128)S(1)} %copy.10.links, f32[20]{0:T(128)S(1)} %copy-done.3, bf16[128,2560]{1,0:T(8,128)(2,1)S(1)} %bitcast.12, bf16[128,2560]{1,0:T(8,128)(2,1)S(1)} %bitcast.13, ...), custom_call_target="tpu_custom_call" | custom-call | tf_op jit(solution)/shard_map/pallas_call | solution.py:457
  178.8 0.5 slice_bitcast_fusion
  179.3 0.8 copy.14
  180.1 0.8 copy.15
  181.0 0.8 copy.16
Async XLA Ops:
  0.6 0.7 copy-start.4
  1.3 0.7 copy-start.3
  1.9 1.1 copy-start
  3.0 1.1 copy-start.1
  4.1 1.1 copy-start.2

commit v3 on v2

--- a/solution.py
+++ b/solution.py
@@ -11,12 +11,12 @@
 BLOCK = 128
 HEAD = 128
 CHUNKS = 10
-AHEAD = 2
+AHEAD = 1
 NEG_FILL = -1e30
-LAG_LO = 5
-LAG_T1 = 3
-LAG_S0 = 4
-LAG_END = 6
+LAG_LO = 3
+LAG_T1 = 2
+LAG_S0 = 3
+LAG_END = 4
 
 
 def body_kernel(

time: 182 us -> 176 us (0.967)
  the two profiles are of different devices: /device:TPU:24 before, /device:TPU:28 now
where the time goes in v3:
time: 176 us; the launch traced here: 175 us
  Pallas kernels  167 us (95%)
  local copies, waits for them, and re-layouts  7.58 us (4%)
    pallas_call x1, Pallas kernels, body(): pl.pallas_call(functools.partial(body_kernel, (n, n_ctx, heads)), out_sha...  167 us
    unnamed x14, local copies, waits for them, and re-layouts  7.07 us

profile of v3, /device:TPU:28, one launch (start us, length us, event | category | flops | bytes accessed | tf_op | source)
XLA Modules:
  0.0 175.4 jit_solution(2095183688730329221)
XLA Ops:
  0.6 0.0 copy-start.4
  0.6 0.6 copy-done.4
  1.3 0.0 copy-start.3
  1.3 0.1 copy.10.links
  1.4 0.6 copy-done.3
  1.9 0.0 copy-start
  1.9 1.1 copy-done
  3.0 0.0 copy-start.1
  3.0 1.1 copy-done.1
  4.1 0.0 copy-start.2
  4.1 1.1 copy-done.2
  5.2 167.2 %shard_map.93 = (bf16[128,2560]{1,0:T(8,128)(2,1)S(1)}, bf16[128,2560]{1,0:T(8,128)(2,1)S(1)}, bf16[128,2560]{1,0:T(8,128)(2,1)S(1)}, f32[8,128]{1,0:T(8,128)S(1)}) custom-call(s32[2,1]{1,0:T(2,128)S(1)} %copy.10.links, f32[20]{0:T(128)S(1)} %copy-done.3, bf16[128,2560]{1,0:T(8,128)(2,1)S(1)} %bitcast.12, bf16[128,2560]{1,0:T(8,128)(2,1)S(1)} %bitcast.13, ...), custom_call_target="tpu_custom_call" | custom-call | tf_op jit(solution)/shard_map/pallas_call | solution.py:457
  172.4 0.5 slice_bitcast_fusion
  172.9 0.8 copy.14
  173.7 0.8 copy.15
  174.6 0.8 copy.16
Async XLA Ops:
  0.6 0.7 copy-start.4
  1.3 0.7 copy-start.3
  1.9 1.1 copy-start
  3.0 1.1 copy-start.1
  4.1 1.1 copy-start.2
